TPU v7x, 512 devices: a whole 4x8x8 slice. The times are simulated.
512 devices in a mesh: section: 4 (over y_lo, core), dp: 4 (over y_hi), expert: 32 (over z, x).
Axes of the slice: x: 4, y: 8 (y_hi: 4, y_lo: 2; y = y_hi * 2 + y_lo), z: 8, core: 2. Of those that a mesh axis runs over, the one named last changes fastest.
Arguments:
- stream: bfloat16 [4, 16384, 2048], P('section', ('dp', 'expert')), may hold values from -60 to 60
- norm_gain: bfloat16 [4, 2048], P('section'), may hold values from 0.29882812 to 3
- gate_probs: float32 [4, 16384, 8], P('section', ('dp', 'expert')), may hold values from 0.02 to 1
- expert_ids: int32 [4, 16384, 8], P('section', ('dp', 'expert')), may hold values from 0 to 127, as said below
- gate_up_weight: bfloat16 [4, 32, 2, 2048, 1024], P('section', 'expert', None, None, 'dp'), may hold values from -0.125 to 0.125
- down_weight: bfloat16 [4, 32, 1024, 2048], P('section', 'expert', 'dp'), may hold values from -0.1875 to 0.1875
Outputs:
- handed: bfloat16 [4, 16384, 2048], P('section', ('dp', 'expert'))
Inputs may be any that keep to these rules, and one draw needn't show every extreme that they name: `expert_ids`: each row names 8 different experts. In the rows of one device each expert below 32 is named by at most 12 rows; in each section one such expert is named by exactly 12 rows in the rows of every device.
All inputs are finite; a program needn't handle non-finite values.
Results may differ from a plain program's by a relative error of at most 0.0077.
Values may be sent and summed in bfloat16 or wider, within the bound.
A program may use at most 128 MiB of HBM per device.

v0:
```python
import jax
import jax.numpy as jnp
from jax import lax
from jax.sharding import PartitionSpec as P

CAP = 12


epsilon = 1e-06


def from_behind(value, axis, steps):
    count = lax.axis_size(axis)
    pairs = [(source, (source + steps) % count) for source in range(count)]
    return lax.ppermute(value, axis, pairs)


def normalize(activations, gain_row):
    widened = activations.astype(jnp.float32)
    inverse_rms = lax.rsqrt(jnp.mean(widened * widened, axis=-1, keepdims=True) + epsilon)
    return (widened * inverse_rms * gain_row.astype(jnp.float32)).astype(jnp.bfloat16)


def slot_tables(gate_probs, expert_ids, held_count, capacity):
    weights = gate_probs / jnp.sum(gate_probs, axis=-1, keepdims=True)
    experts = jnp.arange(held_count, dtype=jnp.int32)
    matches = expert_ids[..., None] == experts
    coefficient = jnp.sum(jnp.where(matches, weights[..., None], jnp.float32(0.0)), axis=-2)
    chosen = jnp.any(matches, axis=-2).astype(jnp.int32)
    position = jnp.cumsum(chosen, axis=-2) - chosen
    places = jnp.arange(capacity, dtype=jnp.int32)
    slot_table = (chosen[..., None] == 1) & (position[..., None] == places)
    return (coefficient, slot_table)


def expert_quarter(slot_rows, gate_up, down_matrix):
    gate_rows = jnp.dot(slot_rows, gate_up[0], preferred_element_type=jnp.float32)
    up_rows = jnp.dot(slot_rows, gate_up[1], preferred_element_type=jnp.float32)
    hidden = (jax.nn.silu(gate_rows) * up_rows).astype(jnp.bfloat16)
    return jnp.dot(hidden, down_matrix, preferred_element_type=jnp.float32).astype(jnp.bfloat16)


def shards(stream, norm_gain, gate_probs, expert_ids, gate_up_weight, down_weight):
    normed = normalize(stream[0], norm_gain[0])
    held_count = lax.axis_size("expert")
    group_count = lax.axis_size("dp")
    coefficient, slot_table = slot_tables(gate_probs[0], expert_ids[0], held_count, CAP)
    slot_onehot = slot_table.astype(jnp.bfloat16)
    packed = jnp.einsum(
        "tec,td->ecd", slot_onehot, normed, preferred_element_type=jnp.float32
    ).astype(jnp.bfloat16)
    gate_up = gate_up_weight[0, 0]
    down_matrix = down_weight[0, 0]
    feature_count = normed.shape[1]
    capacity = packed.shape[1]
    fanned = jnp.broadcast_to(packed[None], (group_count,) + packed.shape)
    fanned = fanned.reshape(group_count * held_count, capacity, feature_count)
    received = lax.all_to_all(fanned, ("dp", "expert"), split_axis=0, concat_axis=0, tiled=True)
    slot_count = received.shape[1]
    partial_rows = expert_quarter(received.reshape(-1, feature_count), gate_up, down_matrix)
    partial_rows = partial_rows.reshape(group_count * held_count, slot_count, feature_count)
    returned = lax.all_to_all(
        partial_rows, ("dp", "expert"), split_axis=0, concat_axis=0, tiled=True
    )
    returned = returned.reshape(group_count, held_count, capacity, feature_count)
    rounded = jnp.sum(returned.astype(jnp.float32), axis=0).astype(jnp.bfloat16)
    expert_sums = lax.optimization_barrier(rounded).astype(jnp.float32)
    shares = slot_table.astype(jnp.float32) * coefficient[..., None]
    mixture = jnp.einsum(
        "tec,ecd->td", shares, expert_sums, precision=lax.Precision.HIGHEST
    ).astype(jnp.bfloat16)
    return from_behind(mixture[None], "section", 1)


def solution(mesh):
    in_specs = (
        P("section", ("dp", "expert"), None),
        P("section", None),
        P("section", ("dp", "expert"), None),
        P("section", ("dp", "expert"), None),
        P("section", "expert", None, None, "dp"),
        P("section", "expert", "dp", None),
    )
    out_specs = P("section", ("dp", "expert"), None)
    return jax.shard_map(shards, mesh=mesh, in_specs=in_specs, out_specs=out_specs, check_vma=False)
```

profile of v0, /device:TPU:1, one launch (start us, length us, event | category | flops | bytes accessed | tf_op | source)
XLA Modules:
  0.0 508.9 jit_solution(4997227206455112746)
XLA Ops:
  0.0 0.0 copy-start
  0.0 0.8 fusion.25
  0.8 0.1 copy.23
  1.0 0.2 reduce_window_sum.11
  1.1 0.1 copy.25
  1.2 0.1 copy.24
  1.3 0.7 mul.50
  2.0 1.2 fusion.4
  3.2 1.7 convolution_convert_fusion.1
  4.9 0.9 copy.26
  5.8 1.1 broadcast_in_dim.18
  6.9 217.3 %all_to_all.10 = bf16[128,12,2048]{2,1,0:T(8,128)(2,1)} all-to-all(bf16[128,12,2048]{2,1,0:T(8,128)(2,1)S(1)} %bitcast.36), channel_id=1, replica_groups=mesh['section'=4,'dp'=4,'expert'=32] {'dp','expert'}, dimensions={0} | all-to-all | bytes 12582912 | tf_op jit(solution)/shard_map/all_to_all | solution.py:58
  224.2 0.0 copy-start.3
  224.2 10.9 %reshape.66 = bf16[1536,2048]{1,0:T(8,128)(2,1)} reshape(bf16[128,12,2048]{2,1,0:T(8,128)(2,1)} %all_to_all.10) | data formatting | bytes 12582912 | tf_op jit(solution)/shard_map/reshape | solution.py:60
  235.0 0.0 copy-done.3
  235.0 5.7 %fusion.10 = f32[1536,256]{1,0:T(8,128)} fusion(bf16[1536,2048]{1,0:T(8,128)(2,1)} %reshape.66, bf16[1,1,2,2048,256]{4,3,2,1,0:T(8,128)(2,1)S(1)} %copy-done.3), kind=kOutput, calls=%fused_computation.15 | convolution fusion | flops 1610612736 | bytes 8912896 | tf_op jit(solution)/shard_map/dot_general | solution.py:37
  240.8 0.0 copy-done
  240.8 12.2 %convolution_convert_fusion = bf16[1536,2048]{1,0:T(8,128)(2,1)} fusion(bf16[1536,2048]{1,0:T(8,128)(2,1)} %reshape.66, f32[1536,256]{1,0:T(8,128)} %fusion.10, bf16[1,1,256,2048]{3,2,1,0:T(8,128)(2,1)S(1)} %copy-done, bf16[1,1,2,2048,256]{4,3,2,1,0:T(8,128)(2,1)S(1)} %copy-done.3), kind=kOutput, calls=%fused_computation | convolution fusion | flops 3226730496 | bytes 16252928 | tf_op jit(solution)/shard_map/dot_general | solution.py:40
  253.0 10.6 %reshape.67 = bf16[128,12,2048]{2,1,0:T(8,128)(2,1)} reshape(bf16[1536,2048]{1,0:T(8,128)(2,1)} %convolution_convert_fusion) | data formatting | bytes 12582912 | tf_op jit(solution)/shard_map/reshape | solution.py:61
  263.6 0.0 copy-start.1
  263.6 0.0 copy-start.2
  263.6 23.3 %all-to-all-start.1 = ((bf16[128,12,2048]{2,1,0:T(8,128)(2,1)}), bf16[128,12,2048]{2,1,0:T(8,128)(2,1)}, u32[]{:S(2)}, u32[]{:S(2)}) async-start(bf16[128,12,2048]{2,1,0:T(8,128)(2,1)} %reshape.67), calls=%async_computation.1 | async-start | bytes 16777216 | tf_op jit(solution)/shard_map/all_to_all | solution.py:62
  286.9 0.0 copy-done.1
  286.9 0.0 copy-done.2
  287.0 205.7 %all-to-all-done.1 = bf16[128,12,2048]{2,1,0:T(8,128)(2,1)} async-done(((bf16[128,12,2048]{2,1,0:T(8,128)(2,1)}), bf16[128,12,2048]{2,1,0:T(8,128)(2,1)}, u32[]{:S(2)}, u32[]{:S(2)}) %all-to-all-start.1) | async-done | bytes 6291488 | tf_op jit(solution)/shard_map/all_to_all | solution.py:62
  492.6 5.7 %reduce_sum.42 = bf16[32,12,2048]{2,1,0:T(8,128)(2,1)S(1)} reduce(bf16[4,32,12,2048]{3,2,1,0:T(8,128)(2,1)} %bitcast.10, bf16[]{:T(256)} %constant.20.clone.1), dimensions={0}, to_apply=%region_5.6 | reduce | flops 2359296 | bytes 7864322 | tf_op jit(solution)/shard_map/reduce_sum | solution.py:66
  498.3 1.8 fusion.2
  500.1 1.9 collective-permute-start
  502.0 6.1 %collective-permute-done = bf16[1,128,2048]{2,1,0:T(8,128)(2,1)S(1)} collective-permute-done((bf16[1,128,2048]{2,1,0:T(8,128)(2,1)S(1)}, bf16[1,128,2048]{2,1,0:T(8,128)(2,1)S(1)}, u32[]{:S(2)}, u32[]{:S(2)}) %collective-permute-start) | collective-permute-done | bytes 524320 | tf_op jit(solution)/shard_map/ppermute | solution.py:15
  508.1 0.8 copy.31
  (6 shorter events, 0.1 us)
Async XLA Ops:
  0.0 240.8 %copy-start = (bf16[1,1,256,2048]{3,2,1,0:T(8,128)(2,1)S(1)}, bf16[1,1,256,2048]{3,2,1,0:T(8,128)(2,1)}, u32[]{:S(2)}) copy-start(bf16[1,1,256,2048]{3,2,1,0:T(8,128)(2,1)} %param.11) | copy-start | bytes 3145732
  224.2 10.9 %copy-start.3 = (bf16[1,1,2,2048,256]{4,3,2,1,0:T(8,128)(2,1)S(1)}, bf16[1,1,2,2048,256]{4,3,2,1,0:T(8,128)(2,1)}, u32[]{:S(2)}) copy-start(bf16[1,1,2,2048,256]{4,3,2,1,0:T(8,128)(2,1)} %param.10) | copy-start | bytes 6291460
  263.6 23.3 %copy-start.1 = (f32[1,128,8]{1,2,0:T(8,128)S(1)}, f32[1,128,8]{1,2,0:T(8,128)}, u32[]{:S(2)}) copy-start(f32[1,128,8]{1,2,0:T(8,128)} %param.8) | copy-start | bytes 12292
  263.6 23.4 %copy-start.2 = (s32[1,128,8]{1,2,0:T(8,128)S(1)}, s32[1,128,8]{1,2,0:T(8,128)}, u32[]{:S(2)}) copy-start(s32[1,128,8]{1,2,0:T(8,128)} %param.9) | copy-start | bytes 12292
  263.6 229.1 %all-to-all-start.1 = ((bf16[128,12,2048]{2,1,0:T(8,128)(2,1)}), bf16[128,12,2048]{2,1,0:T(8,128)(2,1)}, u32[]{:S(2)}, u32[]{:S(2)}) async-start(bf16[128,12,2048]{2,1,0:T(8,128)(2,1)} %reshape.67), calls=%async_computation.1 | async-start | bytes 16777216 | tf_op jit(solution)/shard_map/all_to_all | solution.py:62
  500.1 8.0 %collective-permute-start = (bf16[1,128,2048]{2,1,0:T(8,128)(2,1)S(1)}, bf16[1,128,2048]{2,1,0:T(8,128)(2,1)S(1)}, u32[]{:S(2)}, u32[]{:S(2)}) collective-permute-start(bf16[1,128,2048]{2,1,0:T(8,128)(2,1)S(1)} %fusion.2), channel_id=1, source_target_pairs={{0,128},{128,256},{256,384},{384,0},{1,129},{129,257},{257,385},{3... | collective-permute-start | bytes 1572872 | tf_op jit(solution)/shard_map/ppermute | solution.py:15
where the time goes:
time: 517 us; the launch traced here: 509 us
  blocking collectives  217 us (42%)
  waiting for transfers between devices  212 us (41%)
  starting transfers between devices  25.2 us (5%)
  local copies, waits for them, and re-layouts  24.5 us (5%)
  matrix products  21.4 us (4%)
  other arithmetic  8.65 us (2%)
    all_to_all x1, blocking collectives, shards(): lax.all_to_all(fanned, ('dp', 'expert'), split_axis=0, concat_axis=0, til...  217 us
    all_to_all x1, waiting for transfers between devices, shards(): lax.all_to_all(partial_rows, ('dp', 'expert'), split_axis=0, concat_axis=...  206 us
    all_to_all x1, starting transfers between devices, shards(): lax.all_to_all(partial_rows, ('dp', 'expert'), split_axis=0, concat_axis=...  23.3 us
    dot_general x1, matrix products, expert_quarter(): jnp.dot(hidden, down_matrix, preferred_element_type=jnp.float32)  12.2 us
    reshape x1, local copies, waits for them, and re-layouts, shards(): received.reshape(-1, feature_count)  10.9 us
    reshape x1, local copies, waits for them, and re-layouts, shards(): partial_rows.reshape(group_count * held_count, slot_count, feature_count)  10.6 us
  transfers between devices with their start and end apart: 2, of which 2 were waited for; matrix products, arithmetic and copies ran while one was open for 0% of the time, Pallas kernels for 0%

commit v1 on v0

v1 whole, which is shorter than its diff:
```python
import jax
import jax.numpy as jnp
from jax import lax
from jax.sharding import PartitionSpec as P

CAP = 12


epsilon = 1e-06


def from_behind(value, axis, steps):
    count = lax.axis_size(axis)
    pairs = [(source, (source + steps) % count) for source in range(count)]
    return lax.ppermute(value, axis, pairs)


def along_dp(value, weights):
    sections = lax.axis_size("section")
    groups = lax.axis_size("dp")
    pairs = []
    for section in range(sections):
        for group in range(groups):
            near = (section % 2 == 0) == weights
            other = group ^ 1 if near else groups - 1 - group
            pairs.append((section * groups + group, section * groups + other))
    return lax.ppermute(value, ("section", "dp"), pairs)


def normalize(activations, gain_row):
    widened = activations.astype(jnp.float32)
    inverse_rms = lax.rsqrt(jnp.mean(widened * widened, axis=-1, keepdims=True) + epsilon)
    return (widened * inverse_rms * gain_row.astype(jnp.float32)).astype(jnp.bfloat16)


def slot_tables(expert_ids, held_count, capacity):
    experts = jnp.arange(held_count, dtype=jnp.int32)
    matches = expert_ids[..., None] == experts
    chosen = jnp.any(matches, axis=-2).astype(jnp.int32)
    position = jnp.cumsum(chosen, axis=-2) - chosen
    places = jnp.arange(capacity, dtype=jnp.int32)
    return matches, (chosen[..., None] == 1) & (position[..., None] == places)


def hidden_quarter(rows, gate_up):
    gate_rows = jnp.dot(rows, gate_up[0], preferred_element_type=jnp.float32)
    up_rows = jnp.dot(rows, gate_up[1], preferred_element_type=jnp.float32)
    return (jax.nn.silu(gate_rows) * up_rows).astype(jnp.bfloat16)


def shards(stream, norm_gain, gate_probs, expert_ids, gate_up_weight, down_weight):
    held_count = lax.axis_size("expert")
    gate_up = gate_up_weight[0, 0]
    down_matrix = down_weight[0, 0]
    ids = expert_ids[0]
    normed = normalize(stream[0], norm_gain[0])
    other_normed = along_dp(normed, False)
    other_ids = along_dp(ids, False)
    other_gate_up = along_dp(gate_up, True)
    other_down = along_dp(down_matrix, True)
    matches, slot_table = slot_tables(ids, held_count, CAP)
    _, other_table = slot_tables(other_ids, held_count, CAP)
    weights = gate_probs[0] / jnp.sum(gate_probs[0], axis=-1, keepdims=True)
    coefficient = jnp.sum(jnp.where(matches, weights[..., None], jnp.float32(0.0)), axis=-2)
    feature_count = normed.shape[1]
    packed = jnp.einsum(
        "dtec,dtf->edcf",
        jnp.stack([slot_table, other_table]).astype(jnp.bfloat16),
        jnp.stack([normed, other_normed]),
        preferred_element_type=jnp.float32,
    ).astype(jnp.bfloat16)
    packed = packed.reshape(held_count, 2 * CAP, feature_count)
    received = lax.all_to_all(packed, "expert", split_axis=0, concat_axis=0, tiled=True)
    rows = received.reshape(-1, feature_count)
    hidden = hidden_quarter(rows, gate_up)
    other_hidden = hidden_quarter(rows, other_gate_up)
    halves = jnp.dot(hidden, down_matrix, preferred_element_type=jnp.float32)
    halves = halves + jnp.dot(other_hidden, other_down, preferred_element_type=jnp.float32)
    halves = halves.reshape(held_count, 2, CAP, feature_count)
    other_half = along_dp(halves[:, 1].astype(jnp.bfloat16), False)
    rounded = (halves[:, 0] + other_half.astype(jnp.float32)).astype(jnp.bfloat16)
    returned = lax.all_to_all(rounded, "expert", split_axis=0, concat_axis=0, tiled=True)
    expert_sums = returned.astype(jnp.float32)
    shares = slot_table.astype(jnp.float32) * coefficient[..., None]
    mixture = jnp.einsum(
        "tec,ecd->td", shares, expert_sums, precision=lax.Precision.HIGHEST
    ).astype(jnp.bfloat16)
    return from_behind(mixture[None], "section", 1)


def solution(mesh):
    in_specs = (
        P("section", ("dp", "expert"), None),
        P("section", None),
        P("section", ("dp", "expert"), None),
        P("section", ("dp", "expert"), None),
        P("section", "expert", None, None, "dp"),
        P("section", "expert", "dp", None),
    )
    out_specs = P("section", ("dp", "expert"), None)
    return jax.shard_map(shards, mesh=mesh, in_specs=in_specs, out_specs=out_specs, check_vma=False)
```

time: 517 us -> 262 us (0.51)
  the two profiles are of different devices: /device:TPU:1 before, /device:TPU:48 now
where the time goes in v1:
time: 262 us; the launch traced here: 261 us
  waiting for transfers between devices  169 us (65%)
  starting transfers between devices  39.5 us (15%)
  matrix products  26.5 us (10%)
  local copies, waits for them, and re-layouts  15.9 us (6%)
  other arithmetic  10.4 us (4%)
    all_to_all x1, waiting for transfers between devices, shards(): lax.all_to_all(packed, 'expert', split_axis=0, concat_axis=0, tiled=True)  65.2 us
    all_to_all x1, waiting for transfers between devices, shards(): lax.all_to_all(rounded, 'expert', split_axis=0, concat_axis=0, tiled=True)  48 us
    ppermute x5, waiting for transfers between devices, along_dp(): return lax.ppermute(value, ('section', 'dp'), pairs)  47.1 us
    ppermute x5, starting transfers between devices, along_dp(): return lax.ppermute(value, ('section', 'dp'), pairs)  19.5 us
    all_to_all x1, starting transfers between devices, shards(): lax.all_to_all(packed, 'expert', split_axis=0, concat_axis=0, tiled=True)  12.3 us
    dot_general x1, matrix products, shards(): jnp.dot(other_hidden, other_down, preferred_element_type=jnp.float32)  9.74 us
    ppermute x1, waiting for transfers between devices, from_behind(): return lax.ppermute(value, axis, pairs)  8.57 us
    dot_general x1, matrix products, shards(): halves = jnp.dot(hidden, down_matrix, preferred_element_type=jnp.float32)  7.82 us
  transfers between devices with their start and end apart: 8, of which 5 were waited for; matrix products, arithmetic and copies ran while one was open for 8% of the time, Pallas kernels for 0%

profile of v1, /device:TPU:48, one launch (start us, length us, event | category | flops | bytes accessed | tf_op | source)
XLA Modules:
  0.0 261.3 jit_solution(11852174937355026102)
XLA Ops:
  0.0 7.2 %collective-permute-start.1 = (s32[128,8]{0,1:T(8,128)}, s32[128,8]{0,1:T(8,128)S(1)}, u32[]{:S(2)}, u32[]{:S(2)}) collective-permute-start(s32[128,8]{0,1:T(8,128)} %bitcast.77), channel_id=1, source_target_pairs={{0,96},{32,64},{64,32},{96,0},{128,160},{160,128},{192,224},{224,1... | collective-permute-start | bytes 12296 | tf_op jit(solution)/shard_map/ppermute | solution.py:27
  7.2 0.7 mul.71
  7.9 1.2 fusion.10
  9.1 1.2 fusion.12
  10.3 1.9 collective-permute-start
  12.3 0.7 fusion.41
  13.0 1.2 fusion.14
  14.2 0.1 copy.55
  14.4 0.2 reduce_window_sum.17
  14.6 0.1 copy.57
  14.6 0.1 copy.56
  14.7 0.0 collective-permute-done.1
  14.8 0.1 copy.60
  14.9 0.2 reduce_window_sum.18
  15.1 0.1 copy.62
  15.1 0.1 copy.61
  15.2 0.1 fusion.39
  15.3 9.5 %collective-permute-done = bf16[128,2048]{1,0:T(8,128)(2,1)S(1)} collective-permute-done((bf16[128,2048]{1,0:T(8,128)(2,1)S(1)}, bf16[128,2048]{1,0:T(8,128)(2,1)S(1)}, u32[]{:S(2)}, u32[]{:S(2)}) %collective-permute-start) | collective-permute-done | bytes 524320 | tf_op jit(solution)/shard_map/ppermute | solution.py:27
  24.8 1.0 convolution_convert_fusion
  25.8 3.4 %copy.63 = bf16[32,24,2048]{2,1,0:T(8,128)(2,1)} copy(bf16[32,24,2048]{2,0,1:T(8,128)(2,1)S(1)} %bitcast.72) | data formatting | bytes 6291456 | tf_op jit(solution)/shard_map/reshape | solution.py:72
  29.2 12.3 %all-to-all-start = ((bf16[32,24,2048]{2,1,0:T(8,128)(2,1)}), bf16[32,24,2048]{2,1,0:T(8,128)(2,1)S(1)}, u32[]{:S(2)}, u32[]{:S(2)}) async-start(bf16[32,24,2048]{2,1,0:T(8,128)(2,1)} %copy.63), calls=%async_computation | async-start | bytes 6291456 | tf_op jit(solution)/shard_map/all_to_all | solution.py:73
  41.4 4.4 %collective-permute-start.2 = (bf16[2,2048,256]{2,1,0:T(8,128)(2,1)}, bf16[2,2048,256]{2,1,0:T(8,128)(2,1)}, u32[]{:S(2)}, u32[]{:S(2)}) collective-permute-start(bf16[2,2048,256]{2,1,0:T(8,128)(2,1)} %bitcast.74), channel_id=1, source_target_pairs={{0,32},{32,0},{64,96},{96,64},{128,224},{160,192},{192,160},{224,1... | collective-permute-start | bytes 6291464 | tf_op jit(solution)/shard_map/ppermute | solution.py:27
  45.9 2.5 collective-permute-start.3
  48.4 65.2 %all-to-all-done = bf16[32,24,2048]{2,1,0:T(8,128)(2,1)S(1)} async-done(((bf16[32,24,2048]{2,1,0:T(8,128)(2,1)}), bf16[32,24,2048]{2,1,0:T(8,128)(2,1)S(1)}, u32[]{:S(2)}, u32[]{:S(2)}) %all-to-all-start) | async-done | bytes 3145760 | tf_op jit(solution)/shard_map/all_to_all | solution.py:73
  113.6 3.1 %fusion.21 = f32[768,256]{1,0:T(8,128)} fusion(bf16[768,2048]{1,0:T(8,128)(2,1)S(1)} %bitcast.68, bf16[1,1,2,2048,256]{4,3,2,1,0:T(8,128)(2,1)} %param.10), kind=kOutput, calls=%fused_computation.31 | convolution fusion | flops 805306368 | bytes 4980736 | tf_op jit(solution)/shard_map/dot_general | solution.py:46
  116.6 0.0 collective-permute-done.2
  116.6 3.1 %fusion.15 = f32[768,256]{1,0:T(8,128)} fusion(bf16[768,2048]{1,0:T(8,128)(2,1)S(1)} %bitcast.69, bf16[2,2048,256]{2,1,0:T(8,128)(2,1)} %collective-permute-done.2), kind=kOutput, calls=%fused_computation.24 | convolution fusion | flops 805306368 | bytes 4980736 | tf_op jit(solution)/shard_map/dot_general | solution.py:47
  119.7 7.8 %fusion.9 = f32[768,2048]{1,0:T(8,128)} fusion(bf16[768,2048]{1,0:T(8,128)(2,1)S(1)} %bitcast.70, bf16[1,1,2,2048,256]{4,3,2,1,0:T(8,128)(2,1)} %param.10, f32[768,256]{1,0:T(8,128)} %fusion.21, bf16[1,1,256,2048]{3,2,1,0:T(8,128)(2,1)} %param.11), kind=kOutput, calls=%fused_computation.17 | convolution fusion | flops 1611792384 | bytes 12320768 | tf_op jit(solution)/shard_map/dot_general | solution.py:77
  127.6 0.0 collective-permute-done.3
  127.6 9.7 %convolution_add_fusion = f32[768,2048]{1,0:T(8,128)} fusion(f32[768,2048]{1,0:T(8,128)} %fusion.9, bf16[256,2048]{1,0:T(8,128)(2,1)} %collective-permute-done.3, f32[768,256]{1,0:T(8,128)} %fusion.15, bf16[768,2048]{1,0:T(8,128)(2,1)S(1)} %bitcast.71, bf16[2,2048,256]{2,1,0:T(8,128)(2,1)} %collective-permute-done.2), kind=kOutput, calls=%fused_computation.4 | convolution fusion | flops 1613365248 | bytes 18612224 | tf_op jit(solution)/shard_map/dot_general | solution.py:78
  137.3 7.8 %reshape.113 = f32[32,2,12,2048]{3,2,1,0:T(8,128)} reshape(f32[768,2048]{1,0:T(8,128)} %convolution_add_fusion) | data formatting | bytes 12582912 | tf_op jit(solution)/shard_map/reshape | solution.py:79
  145.1 2.5 fusion.4
  147.6 0.9 copy.64
  148.5 3.5 %collective-permute-start.4 = (bf16[32,12,2048]{2,0,1:T(8,128)(2,1)S(1)}, bf16[32,12,2048]{2,0,1:T(8,128)(2,1)S(1)}, u32[]{:S(2)}, u32[]{:S(2)}) collective-permute-start(bf16[32,12,2048]{2,0,1:T(8,128)(2,1)S(1)} %copy.64), channel_id=1, source_target_pairs={{0,96},{32,64},{64,32},{96,0},{128,160},{160,128},{192,224},{224,1... | collective-permute-start | bytes 4718600 | tf_op jit(solution)/shard_map/ppermute | solution.py:27
  151.9 37.6 %collective-permute-done.4 = bf16[32,12,2048]{2,0,1:T(8,128)(2,1)S(1)} collective-permute-done((bf16[32,12,2048]{2,0,1:T(8,128)(2,1)S(1)}, bf16[32,12,2048]{2,0,1:T(8,128)(2,1)S(1)}, u32[]{:S(2)}, u32[]{:S(2)}) %collective-permute-start.4) | collective-permute-done | bytes 1572896 | tf_op jit(solution)/shard_map/ppermute | solution.py:27
  189.6 4.7 %fusion.1 = bf16[32,12,2048]{2,1,0:T(8,128)(2,1)} fusion(f32[32,2,12,2048]{3,2,1,0:T(8,128)} %reshape.113, bf16[32,12,2048]{2,0,1:T(8,128)(2,1)S(1)} %collective-permute-done.4), kind=kLoop, calls=%fused_computation.3 | loop fusion | flops 2359296 | bytes 6291456 | tf_op jit(solution)/shard_map/convert_element_type | solution.py:81
  194.3 0.0 copy-start
  194.3 0.0 copy-start.1
  194.3 5.8 %all-to-all-start.1 = ((bf16[32,12,2048]{2,1,0:T(8,128)(2,1)}), bf16[32,12,2048]{2,1,0:T(8,128)(2,1)S(1)}, u32[]{:S(2)}, u32[]{:S(2)}) async-start(bf16[32,12,2048]{2,1,0:T(8,128)(2,1)} %fusion.1), calls=%async_computation.1 | async-start | bytes 4194304 | tf_op jit(solution)/shard_map/all_to_all | solution.py:82
  200.1 0.0 copy-done
  200.2 0.0 copy-done.1
  200.2 48.0 %all-to-all-done.1 = bf16[32,12,2048]{2,1,0:T(8,128)(2,1)S(1)} async-done(((bf16[32,12,2048]{2,1,0:T(8,128)(2,1)}), bf16[32,12,2048]{2,1,0:T(8,128)(2,1)S(1)}, u32[]{:S(2)}, u32[]{:S(2)}) %all-to-all-start.1) | async-done | bytes 1572896 | tf_op jit(solution)/shard_map/all_to_all | solution.py:82
  248.2 1.8 fusion.3
  250.0 1.9 collective-permute-start.5
  251.9 8.6 %collective-permute-done.5 = bf16[1,128,2048]{2,1,0:T(8,128)(2,1)S(1)} collective-permute-done((bf16[1,128,2048]{2,1,0:T(8,128)(2,1)S(1)}, bf16[1,128,2048]{2,1,0:T(8,128)(2,1)S(1)}, u32[]{:S(2)}, u32[]{:S(2)}) %collective-permute-start.5) | collective-permute-done | bytes 524320 | tf_op jit(solution)/shard_map/ppermute | solution.py:15
  260.5 0.8 copy.76
  (9 shorter events, 0.1 us)
Async XLA Ops:
  0.0 14.7 %collective-permute-start.1 = (s32[128,8]{0,1:T(8,128)}, s32[128,8]{0,1:T(8,128)S(1)}, u32[]{:S(2)}, u32[]{:S(2)}) collective-permute-start(s32[128,8]{0,1:T(8,128)} %bitcast.77), channel_id=1, source_target_pairs={{0,96},{32,64},{64,32},{96,0},{128,160},{160,128},{192,224},{224,1... | collective-permute-start | bytes 12296 | tf_op jit(solution)/shard_map/ppermute | solution.py:27
  10.3 14.4 %collective-permute-start = (bf16[128,2048]{1,0:T(8,128)(2,1)S(1)}, bf16[128,2048]{1,0:T(8,128)(2,1)S(1)}, u32[]{:S(2)}, u32[]{:S(2)}) collective-permute-start(bf16[128,2048]{1,0:T(8,128)(2,1)S(1)} %fusion.12), channel_id=1, source_target_pairs={{0,96},{32,64},{64,32},{96,0},{128,160},{160,128},{192,224},{224,1... | collective-permute-start | bytes 1572872 | tf_op jit(solution)/shard_map/ppermute | solution.py:27
  29.2 84.4 %all-to-all-start = ((bf16[32,24,2048]{2,1,0:T(8,128)(2,1)}), bf16[32,24,2048]{2,1,0:T(8,128)(2,1)S(1)}, u32[]{:S(2)}, u32[]{:S(2)}) async-start(bf16[32,24,2048]{2,1,0:T(8,128)(2,1)} %copy.63), calls=%async_computation | async-start | bytes 6291456 | tf_op jit(solution)/shard_map/all_to_all | solution.py:73
  41.4 75.2 %collective-permute-start.2 = (bf16[2,2048,256]{2,1,0:T(8,128)(2,1)}, bf16[2,2048,256]{2,1,0:T(8,128)(2,1)}, u32[]{:S(2)}, u32[]{:S(2)}) collective-permute-start(bf16[2,2048,256]{2,1,0:T(8,128)(2,1)} %bitcast.74), channel_id=1, source_target_pairs={{0,32},{32,0},{64,96},{96,64},{128,224},{160,192},{192,160},{224,1... | collective-permute-start | bytes 6291464 | tf_op jit(solution)/shard_map/ppermute | solution.py:27
  45.9 81.7 %collective-permute-start.3 = (bf16[256,2048]{1,0:T(8,128)(2,1)}, bf16[256,2048]{1,0:T(8,128)(2,1)}, u32[]{:S(2)}, u32[]{:S(2)}) collective-permute-start(bf16[256,2048]{1,0:T(8,128)(2,1)} %bitcast.73), channel_id=1, source_target_pairs={{0,32},{32,0},{64,96},{96,64},{128,224},{160,192},{192,160},{224,1... | collective-permute-start | bytes 3145736 | tf_op jit(solution)/shard_map/ppermute | solution.py:27
  148.5 41.1 %collective-permute-start.4 = (bf16[32,12,2048]{2,0,1:T(8,128)(2,1)S(1)}, bf16[32,12,2048]{2,0,1:T(8,128)(2,1)S(1)}, u32[]{:S(2)}, u32[]{:S(2)}) collective-permute-start(bf16[32,12,2048]{2,0,1:T(8,128)(2,1)S(1)} %copy.64), channel_id=1, source_target_pairs={{0,96},{32,64},{64,32},{96,0},{128,160},{160,128},{192,224},{224,1... | collective-permute-start | bytes 4718600 | tf_op jit(solution)/shard_map/ppermute | solution.py:27
  194.3 5.8 %copy-start = (f32[1,128,8]{1,2,0:T(8,128)S(1)}, f32[1,128,8]{1,2,0:T(8,128)}, u32[]{:S(2)}) copy-start(f32[1,128,8]{1,2,0:T(8,128)} %param.8) | copy-start | bytes 12292
  194.3 5.9 %copy-start.1 = (s32[1,128,8]{1,2,0:T(8,128)S(1)}, s32[1,128,8]{1,2,0:T(8,128)}, u32[]{:S(2)}) copy-start(s32[1,128,8]{1,2,0:T(8,128)} %param.9) | copy-start | bytes 12292
  194.3 53.9 %all-to-all-start.1 = ((bf16[32,12,2048]{2,1,0:T(8,128)(2,1)}), bf16[32,12,2048]{2,1,0:T(8,128)(2,1)S(1)}, u32[]{:S(2)}, u32[]{:S(2)}) async-start(bf16[32,12,2048]{2,1,0:T(8,128)(2,1)} %fusion.1), calls=%async_computation.1 | async-start | bytes 4194304 | tf_op jit(solution)/shard_map/all_to_all | solution.py:82
  250.0 10.5 %collective-permute-start.5 = (bf16[1,128,2048]{2,1,0:T(8,128)(2,1)S(1)}, bf16[1,128,2048]{2,1,0:T(8,128)(2,1)S(1)}, u32[]{:S(2)}, u32[]{:S(2)}) collective-permute-start(bf16[1,128,2048]{2,1,0:T(8,128)(2,1)S(1)} %fusion.3), channel_id=1, source_target_pairs={{0,128},{128,256},{256,384},{384,0},{1,129},{129,257},{257,385},{3... | collective-permute-start | bytes 1572872 | tf_op jit(solution)/shard_map/ppermute | solution.py:15

commit v2 on v0

v2 whole, which is shorter than its diff:
```python
import functools

import jax
import jax.numpy as jnp
import numpy as np
from jax import lax
from jax.experimental import pallas as pl
from jax.experimental.pallas import tpu as pltpu
from jax.sharding import PartitionSpec as P

MESH = pl.DeviceIdType.MESH
CAP = 12
EPSILON = 1e-06
NZ = 8
NX = 4
NF = 4
SLAB = CAP * NF
F32 = jnp.float32
BF16 = jnp.bfloat16


def mm(a, b):
    return jnp.dot(a, b, preferred_element_type=F32)


def kernel(
    stream, gain, probs, ids, gu_hbm, dn_hbm, unpack, repack, out,
    raw, code, coef, grid, stacked, psend, drec, gu, dn, mine, ysend, yrecv, zsend, rec,
    shares, osend, hop,
    raw_ss, raw_rs, d_ss, d_rs, w_ss, w_rs, l_sem, y_ss, y_rs, s_ss, s_rs, h_ss, h_rs,
):
    tokens, features = stream.shape
    width = features // NF
    held = NZ * NX
    section, group, me = lax.axis_index("section"), lax.axis_index("dp"), lax.axis_index("expert")
    z, x = me // NX, me % NX
    core = section % 2
    beside = group + 1 - 2 * (group % 2)
    across = 3 - group
    row_mate = core * beside + (1 - core) * across
    weight_mate = (1 - core) * beside + core * across
    ahead, behind = (section + 1) % 4, (section + 3) % 4

    def peer(step):
        turn = step // NX
        zs = (z + 4 + (1 - 2 * (turn % 2)) * ((turn + 1) // 2)) % NZ
        return zs, zs * NX + (x + step % NX) % NX

    last = held - NX

    barrier = pltpu.get_barrier_semaphore()
    pl.semaphore_signal(barrier, inc=1, device_id={"dp": row_mate}, device_id_type=MESH)
    pl.semaphore_signal(barrier, inc=1, device_id={"dp": weight_mate}, device_id_type=MESH)
    pl.semaphore_signal(barrier, inc=1, device_id={"section": behind}, device_id_type=MESH)

    def greet(j, carry):
        pl.semaphore_signal(
            barrier, inc=1, device_id={"expert": (me + j) % held}, device_id_type=MESH
        )
        return carry

    lax.fori_loop(1, held, greet, 0)
    own_gu = pltpu.make_async_copy(gu_hbm, gu.at[0], l_sem.at[0])
    own_gu.start()
    own_dn = pltpu.make_async_copy(dn_hbm, dn.at[0], l_sem.at[1])
    own_dn.start()

    wide = stream[...].astype(F32)
    inverse = lax.rsqrt(jnp.mean(wide * wide, axis=-1, keepdims=True) + EPSILON)
    raw[0] = (wide * inverse * gain[...].astype(F32)).astype(BF16)

    expert_iota = lax.broadcasted_iota(jnp.int32, (held, tokens), 0)
    weights = probs[...] / jnp.sum(probs[...], axis=0, keepdims=True)
    chosen = jnp.zeros((held, tokens), F32)
    total = jnp.zeros((held, tokens), F32)
    for k in range(ids.shape[0]):
        match = ids[k : k + 1, :] == expert_iota
        chosen = chosen + jnp.where(match, 1.0, 0.0)
        total = total + jnp.where(match, weights[k : k + 1, :], 0.0)
    earlier = lax.broadcasted_iota(jnp.int32, (tokens, tokens), 0) < lax.broadcasted_iota(
        jnp.int32, (tokens, tokens), 1
    )
    position = mm(chosen.astype(BF16), jnp.where(earlier, 1.0, 0.0).astype(BF16))
    code[0] = jnp.where(chosen > 0.5, position, -1.0)
    coef[...] = total

    pl.semaphore_wait(barrier, held - 1 + 3)

    def to_mate(src, dst, k):
        return pltpu.make_async_remote_copy(
            src_ref=src, dst_ref=dst, send_sem=raw_ss.at[k], recv_sem=raw_rs.at[k],
            device_id={"dp": row_mate}, device_id_type=MESH,
        )

    raw_copy = to_mate(raw.at[0], raw.at[1], 0)
    code_copy = to_mate(code.at[0], code.at[1], 1)
    code_copy.start()
    raw_copy.start()

    row_iota = lax.broadcasted_iota(jnp.int32, (SLAB, tokens), 0)
    row_block = jnp.where(row_iota >= CAP, 1, 0)
    for f in range(2, NF):
        row_block = row_block + jnp.where(row_iota >= CAP * f, 1, 0)
    row_slot = (row_iota - CAP * row_block).astype(F32)

    def dispatch_copy(d, step):
        _, other = peer(step)
        return pltpu.make_async_remote_copy(
            src_ref=psend.at[d, other], dst_ref=drec.at[me, d],
            send_sem=d_ss.at[d, step], recv_sem=d_rs.at[d, me],
            device_id={"expert": other}, device_id_type=MESH,
        )

    def dispatch(d):
        def fill(e, carry):
            hit = code[d, pl.ds(e, 1), :] == row_slot
            for f in range(NF):
                grid[pl.ds(pl.multiple_of(e * SLAB, SLAB), SLAB), f * tokens : (f + 1) * tokens] = (
                    jnp.where(hit, jnp.where(row_block == f, 1.0, 0.0), 0.0).astype(BF16)
                )
            return carry

        lax.fori_loop(0, held, fill, 0)
        for f in range(NF):
            stacked[f * tokens : (f + 1) * tokens, :] = raw[d, :, f * width : (f + 1) * width]

        def pack(j, carry):
            rows = pl.ds(pl.multiple_of(j * 8 * SLAB, 8 * SLAB), 8 * SLAB)
            slabs = mm(grid[rows, :], stacked[...]).astype(BF16)
            psend[d, pl.ds(j * 8, 8)] = slabs.reshape(8, SLAB, width)
            return carry

        lax.fori_loop(0, held // 8, pack, 0)

        def send(step, carry):
            dispatch_copy(d, step).start()
            return carry

        lax.fori_loop(0, last, send, 0)
        lax.fori_loop(last + 1, held, send, 0)
        drec[me, d] = psend[d, me]

    dispatch(0)
    raw_copy.wait()
    code_copy.wait()

    def to_weight_mate(src, dst, k):
        return pltpu.make_async_remote_copy(
            src_ref=src, dst_ref=dst, send_sem=w_ss.at[k], recv_sem=w_rs.at[k],
            device_id={"dp": weight_mate}, device_id_type=MESH,
        )

    gu_copy = to_weight_mate(gu_hbm, gu.at[1], 0)
    dn_copy = to_weight_mate(dn_hbm, dn.at[1], 1)
    gu_copy.start()
    dn_copy.start()
    dispatch(1)

    def share(e, carry):
        hit = code[0, pl.ds(e, 1), :] == row_slot
        value = coef[pl.ds(e, 1), :]
        high = value.astype(BF16).astype(F32)
        low = value - high
        rows = pl.ds(pl.multiple_of(e * SLAB, SLAB), SLAB)
        for f in range(NF):
            here = jnp.where(hit, jnp.where(row_block == f, 1.0, 0.0), 0.0)
            base = 2 * f * tokens
            shares[rows, base : base + tokens] = (here * high).astype(BF16)
            shares[rows, base + tokens : base + 2 * tokens] = (here * low).astype(BF16)
        return carry

    lax.fori_loop(0, held, share, 0)

    own_gu.wait()
    own_dn.wait()
    gu_copy.wait()
    dn_copy.wait()

    def y_copy(turn):
        return pltpu.make_async_remote_copy(
            src_ref=ysend.at[turn], dst_ref=yrecv.at[turn],
            send_sem=y_ss.at[turn], recv_sem=y_rs.at[turn],
            device_id={"dp": row_mate}, device_id_type=MESH,
        )

    def arrived(other):
        for d in range(2):
            pltpu.make_async_remote_copy(
                src_ref=psend.at[d, other], dst_ref=drec.at[other, d],
                send_sem=d_ss.at[d, 0], recv_sem=d_rs.at[d, other],
                device_id={"expert": other}, device_id_type=MESH,
            ).wait_recv()

    per_z = NX * CAP

    def expert_block(turn, own):
        zs, _ = peer(turn * NX)
        for k in range(1 if own else 0, NX):
            arrived(peer(turn * NX + k)[1])
        block = drec[pl.ds(zs * NX, NX)].reshape(NX * 2 * SLAB, width)
        rows = mm(unpack[...], block).astype(BF16)
        result = jnp.zeros((2 * per_z, features), F32)
        for half in range(2):
            gate = jnp.zeros((2 * per_z, gu.shape[3]), F32)
            up = jnp.zeros((2 * per_z, gu.shape[3]), F32)
            for f in range(NF):
                part = rows[f * 2 * per_z : (f + 1) * 2 * per_z, :]
                gate = gate + mm(part, gu[half, 0, f * width : (f + 1) * width, :])
                up = up + mm(part, gu[half, 1, f * width : (f + 1) * width, :])
            hidden = (gate / (1.0 + jnp.exp(-gate)) * up).astype(BF16)
            result = result + mm(hidden, dn[half])
        mine[turn] = result[:per_z]
        ysend[turn] = result[per_z:].astype(BF16)
        y_copy(turn).start()

    def back_copy(step):
        _, other = peer(step)
        return pltpu.make_async_remote_copy(
            src_ref=zsend.at[step // NX, other % NX], dst_ref=rec.at[me],
            send_sem=s_ss.at[step], recv_sem=s_rs.at[me],
            device_id={"expert": other}, device_id_type=MESH,
        )

    def give_back(turn, own):
        y_copy(turn).wait_recv()
        summed = (mine[turn] + yrecv[turn].astype(F32)).astype(BF16)
        tall = jnp.concatenate(
            [summed[:, f * width : (f + 1) * width] for f in range(NF)], axis=0
        )
        zsend[turn] = mm(repack[...], tall).astype(BF16).reshape(NX, SLAB, width)
        for k in range(1 if own else 0, NX):
            back_copy(turn * NX + k).start()
        if own:
            rec[me] = zsend[turn, x]

    expert_block(0, False)
    expert_block(1, False)

    def steady(turn, carry):
        expert_block(turn, False)
        give_back(turn - 2, False)
        return carry

    lax.fori_loop(2, NZ - 1, steady, 0)
    expert_block(NZ - 1, True)
    give_back(NZ - 3, False)
    give_back(NZ - 2, False)
    give_back(NZ - 1, True)

    def returned(j, carry):
        other = (me + j) % held
        pltpu.make_async_remote_copy(
            src_ref=zsend.at[0, 0], dst_ref=rec.at[other],
            send_sem=s_ss.at[0], recv_sem=s_rs.at[other],
            device_id={"expert": other}, device_id_type=MESH,
        ).wait_recv()
        return carry

    lax.fori_loop(1, held, returned, 0)

    def hop_copy(f):
        return pltpu.make_async_remote_copy(
            src_ref=osend.at[f], dst_ref=hop.at[f], send_sem=h_ss.at[f], recv_sem=h_rs.at[f],
            device_id={"section": ahead}, device_id_type=MESH,
        )

    everything = rec[...].reshape(held * SLAB, width)
    for f in range(NF):
        both = lax.dot_general(
            shares[:, 2 * f * tokens : 2 * (f + 1) * tokens], everything,
            (((0,), (0,)), ((), ())), preferred_element_type=F32,
        )
        osend[f] = (both[:tokens] + both[tokens:]).astype(BF16)
        hop_copy(f).start()

    def left(step, carry):
        for d in range(2):
            dispatch_copy(d, step).wait_send()
        back_copy(step).wait_send()
        return carry

    lax.fori_loop(0, last, left, 0)
    lax.fori_loop(last + 1, held, left, 0)

    def left_along_y(turn, carry):
        y_copy(turn).wait_send()
        return carry

    lax.fori_loop(0, NZ, left_along_y, 0)
    for f in range(NF):
        hop_copy(f).wait()
        out[:, f * width : (f + 1) * width] = hop[f]


def moves():
    per_z = NX * CAP
    unpack = np.zeros((NF * 2 * per_z, NX * 2 * SLAB), np.float32)
    repack = np.zeros((NX * SLAB, NX * SLAB), np.float32)
    for f in range(NF):
        for xs in range(NX):
            for c in range(CAP):
                for d in range(2):
                    unpack[((f * 2 + d) * NX + xs) * CAP + c, ((xs * 2 + d) * NF + f) * CAP + c] = 1
                repack[(xs * NF + f) * CAP + c, (f * NX + xs) * CAP + c] = 1
    return jnp.asarray(unpack, BF16), jnp.asarray(repack, BF16)


def shards(stream, norm_gain, gate_probs, expert_ids, gate_up_weight, down_weight):
    tokens, features = stream.shape[1:]
    held = NZ * NX
    width = features // NF
    units = gate_up_weight.shape[4]
    unpack, repack = moves()
    vmem = pl.BlockSpec(memory_space=pltpu.VMEM)
    anywhere = pl.BlockSpec(memory_space=pl.ANY)
    dma = pltpu.SemaphoreType.DMA
    result = pl.pallas_call(
        kernel,
        out_shape=jax.ShapeDtypeStruct((tokens, features), BF16),
        in_specs=[vmem, vmem, vmem, vmem, anywhere, anywhere, vmem, vmem],
        out_specs=vmem,
        scratch_shapes=[
            pltpu.VMEM((2, tokens, features), BF16),
            pltpu.VMEM((2, held, tokens), F32),
            pltpu.VMEM((held, tokens), F32),
            pltpu.VMEM((held * SLAB, NF * tokens), BF16),
            pltpu.VMEM((NF * tokens, width), BF16),
            pltpu.VMEM((2, held, SLAB, width), BF16),
            pltpu.VMEM((held, 2, SLAB, width), BF16),
            pltpu.VMEM((2, 2, features, units), BF16),
            pltpu.VMEM((2, units, features), BF16),
            pltpu.VMEM((NZ, NX * CAP, features), F32),
            pltpu.VMEM((NZ, NX * CAP, features), BF16),
            pltpu.VMEM((NZ, NX * CAP, features), BF16),
            pltpu.VMEM((NZ, NX, SLAB, width), BF16),
            pltpu.VMEM((held, SLAB, width), BF16),
            pltpu.VMEM((held * SLAB, 2 * NF * tokens), BF16),
            pltpu.VMEM((NF, tokens, width), BF16),
            pltpu.VMEM((NF, tokens, width), BF16),
            dma((2,)), dma((2,)), dma((2, held)), dma((2, held)), dma((2,)), dma((2,)),
            dma((2,)), dma((NZ,)), dma((NZ,)), dma((held,)), dma((held,)),
            dma((NF,)), dma((NF,)),
        ],
        compiler_params=pltpu.CompilerParams(
            collective_id=0, has_side_effects=True, vmem_limit_bytes=56 << 20
        ),
        name="routed",
    )(
        stream[0], norm_gain, gate_probs[0].T, expert_ids[0].T,
        gate_up_weight[0, 0], down_weight[0, 0], unpack, repack,
    )
    return result[None]


def solution(mesh):
    in_specs = (
        P("section", ("dp", "expert"), None),
        P("section", None),
        P("section", ("dp", "expert"), None),
        P("section", ("dp", "expert"), None),
        P("section", "expert", None, None, "dp"),
        P("section", "expert", "dp", None),
    )
    out_specs = P("section", ("dp", "expert"), None)
    return jax.shard_map(shards, mesh=mesh, in_specs=in_specs, out_specs=out_specs, check_vma=False)
```

time: 517 us -> 167 us (0.32); the launches traced: 509 us -> 167 us
  blocking collectives: 217 us -> 0 us
  waiting for transfers between devices: 212 us -> 0 us
  Pallas kernels: 0 us -> 165 us
  starting transfers between devices: 25.2 us -> 0 us
  local copies, waits for them, and re-layouts: 24.5 us -> 1.88 us
  matrix products: 21.4 us -> 0 us
  other arithmetic: 8.65 us -> 0 us
    all_to_all x1 -> x0, blocking collectives: 217 us -> none  [shards(): lax.all_to_all(fanned, ('dp', 'expert'), split_axis=0, concat_axis=0, til...]
    all_to_all x1 -> x0, waiting for transfers between devices: 206 us -> none  [shards(): lax.all_to_all(partial_rows, ('dp', 'expert'), split_axis=0, concat_axis=...]
    pallas_call x0 -> x1, Pallas kernels: none -> 165 us  [shards(): pl.pallas_call(kernel, out_shape=jax.ShapeDtypeStruct((tokens, features),...]
    all_to_all x1 -> x0, starting transfers between devices: 23.3 us -> none  [shards(): lax.all_to_all(partial_rows, ('dp', 'expert'), split_axis=0, concat_axis=...]
    reshape x2 -> x0, local copies, waits for them, and re-layouts: 21.4 us -> none  [the longest x1 10.9 us: shards(): received.reshape(-1, feature_count)]
    dot_general x4 -> x0, matrix products: 21.4 us -> none  [the longest x1 12.2 us: expert_quarter(): jnp.dot(hidden, down_matrix, preferred_element_type=jnp.float32)]
    reduce_sum x4 -> x0, other arithmetic: 6.93 us -> none  [the longest x1 5.66 us: shards(): rounded = jnp.sum(returned.astype(jnp.float32), axis=0).astype(jnp.bfloat16)]
    ppermute x1 -> x0, waiting for transfers between devices: 6.1 us -> none  [from_behind(): return lax.ppermute(value, axis, pairs)]
  transfers between devices with their start and end apart: 2 -> 0, of which waited for: 2 -> 0; matrix products, arithmetic and copies ran while one was open for 0% -> 0% of each run, Pallas kernels for 0% -> 0%
where the time goes in v2:
time: 167 us
  Pallas kernels  165 us (99%)
  local copies, waits for them, and re-layouts  1.88 us (1%)
    pallas_call x1, Pallas kernels, shards(): pl.pallas_call(kernel, out_shape=jax.ShapeDtypeStruct((tokens, features),...  165 us

profile of v2, /device:TPU:1, one launch (start us, length us, event | category | flops | bytes accessed | tf_op | source)
XLA Modules:
  0.0 167.0 jit_solution(5062580093748573620)
XLA Ops:
  0.0 165.1 %routed.1 = bf16[128,2048]{1,0:T(8,128)(2,1)} custom-call(bf16[128,2048]{1,0:T(8,128)(2,1)} %bitcast.13, bf16[1,2048]{1,0:T(2,128)(2,1)} %gain.1, f32[8,128]{1,0:T(8,128)} %bitcast.14, s32[8,128]{1,0:T(8,128)} %bitcast.15, bf16[2,2048,256]{2,1,0:T(8,128)(2,1)} %bitcast.11, bf16[256,2048]{1,0:T(8,128)(2,1)} %bitcast.12, ...), custom_call_target="tpu_custom_call" | custom-call | tf_op jit(solution)/shard_map/routed/pallas_call | solution.py:317
  165.1 1.9 %copy.10 = bf16[1,128,2048]{2,1,0:T(8,128)(2,1)} copy(bf16[1,128,2048]{2,1,0:T(8,128)(2,1)} %bitcast.10) | data formatting | bytes 1048576

commit v3 on v2

--- a/solution.py
+++ b/solution.py
@@ -25,9 +25,9 @@
 
 def kernel(
     stream, gain, probs, ids, gu_hbm, dn_hbm, unpack, repack, out,
-    raw, code, coef, grid, stacked, psend, drec, gu, dn, mine, ysend, yrecv, zsend, rec,
+    raw, code, coef, grid, stacked, psend, drec, gu, dn, rows, mine, hid, ysend, yrecv, zsend, rec,
     shares, osend, hop,
-    raw_ss, raw_rs, d_ss, d_rs, w_ss, w_rs, l_sem, y_ss, y_rs, s_ss, s_rs, h_ss, h_rs,
+    raw_ss, raw_rs, d_ss, d_rs, w_ss, w_rs, l_sem, y_ss, y_rs, s_ss, s_rs, h_ss, h_rs, plane_sem,
 ):
     tokens, features = stream.shape
     width = features // NF
@@ -53,13 +53,10 @@
     pl.semaphore_signal(barrier, inc=1, device_id={"dp": weight_mate}, device_id_type=MESH)
     pl.semaphore_signal(barrier, inc=1, device_id={"section": behind}, device_id_type=MESH)
 
-    def greet(j, carry):
-        pl.semaphore_signal(
-            barrier, inc=1, device_id={"expert": (me + j) % held}, device_id_type=MESH
-        )
-        return carry
-
-    lax.fori_loop(1, held, greet, 0)
+    along_x = [z * NX + (x + k) % NX for k in range(1, NX)]
+    along_z = [(z + k) % NZ * NX + x for k in range(1, NZ)]
+    for other in along_x + along_z:
+        pl.semaphore_signal(barrier, inc=1, device_id={"expert": other}, device_id_type=MESH)
     own_gu = pltpu.make_async_copy(gu_hbm, gu.at[0], l_sem.at[0])
     own_gu.start()
     own_dn = pltpu.make_async_copy(dn_hbm, dn.at[0], l_sem.at[1])
@@ -84,7 +81,7 @@
     code[0] = jnp.where(chosen > 0.5, position, -1.0)
     coef[...] = total
 
-    pl.semaphore_wait(barrier, held - 1 + 3)
+    pl.semaphore_wait(barrier, len(along_x + along_z) + 3)
 
     def to_mate(src, dst, k):
         return pltpu.make_async_remote_copy(
@@ -96,6 +93,23 @@
     code_copy = to_mate(code.at[0], code.at[1], 1)
     code_copy.start()
     raw_copy.start()
+
+    def to_weight_mate(src, dst, k):
+        return pltpu.make_async_remote_copy(
+            src_ref=src, dst_ref=dst, send_sem=w_ss.at[k], recv_sem=w_rs.at[k],
+            device_id={"dp": weight_mate}, device_id_type=MESH,
+        )
+
+    weight_copies = [
+        to_weight_mate(gu.at[0, 0], gu.at[1, 0], 0),
+        to_weight_mate(gu.at[0, 1], gu.at[1, 1], 1),
+        to_weight_mate(dn.at[0], dn.at[1], 2),
+    ]
+    own_gu.wait()
+    own_dn.wait()
+    weight_copies[0].start()
+    for other in along_x:
+        pl.semaphore_signal(plane_sem, inc=1, device_id={"expert": other}, device_id_type=MESH)
 
     row_iota = lax.broadcasted_iota(jnp.int32, (SLAB, tokens), 0)
     row_block = jnp.where(row_iota >= CAP, 1, 0)
@@ -125,12 +139,15 @@
             stacked[f * tokens : (f + 1) * tokens, :] = raw[d, :, f * width : (f + 1) * width]
 
         def pack(j, carry):
-            rows = pl.ds(pl.multiple_of(j * 8 * SLAB, 8 * SLAB), 8 * SLAB)
-            slabs = mm(grid[rows, :], stacked[...]).astype(BF16)
+            part = pl.ds(pl.multiple_of(j * 8 * SLAB, 8 * SLAB), 8 * SLAB)
+            slabs = mm(grid[part, :], stacked[...]).astype(BF16)
             psend[d, pl.ds(j * 8, 8)] = slabs.reshape(8, SLAB, width)
             return carry
 
         lax.fori_loop(0, held // 8, pack, 0)
+
+        if d == 0:
+            pl.semaphore_wait(plane_sem, len(along_x))
 
         def send(step, carry):
             dispatch_copy(d, step).start()
@@ -144,16 +161,8 @@
     raw_copy.wait()
     code_copy.wait()
 
-    def to_weight_mate(src, dst, k):
-        return pltpu.make_async_remote_copy(
-            src_ref=src, dst_ref=dst, send_sem=w_ss.at[k], recv_sem=w_rs.at[k],
-            device_id={"dp": weight_mate}, device_id_type=MESH,
-        )
-
-    gu_copy = to_weight_mate(gu_hbm, gu.at[1], 0)
-    dn_copy = to_weight_mate(dn_hbm, dn.at[1], 1)
-    gu_copy.start()
-    dn_copy.start()
+    weight_copies[1].start()
+    weight_copies[2].start()
     dispatch(1)
 
     def share(e, carry):
@@ -161,20 +170,16 @@
         value = coef[pl.ds(e, 1), :]
         high = value.astype(BF16).astype(F32)
         low = value - high
-        rows = pl.ds(pl.multiple_of(e * SLAB, SLAB), SLAB)
+        part = pl.ds(pl.multiple_of(e * SLAB, SLAB), SLAB)
         for f in range(NF):
             here = jnp.where(hit, jnp.where(row_block == f, 1.0, 0.0), 0.0)
             base = 2 * f * tokens
-            shares[rows, base : base + tokens] = (here * high).astype(BF16)
-            shares[rows, base + tokens : base + 2 * tokens] = (here * low).astype(BF16)
+            shares[part, base : base + tokens] = (here * high).astype(BF16)
+            shares[part, base + tokens : base + 2 * tokens] = (here * low).astype(BF16)
         return carry
 
     lax.fori_loop(0, held, share, 0)
 
-    own_gu.wait()
-    own_dn.wait()
-    gu_copy.wait()
-    dn_copy.wait()
 
     def y_copy(turn):
         return pltpu.make_async_remote_copy(
@@ -183,35 +188,49 @@
             device_id={"dp": row_mate}, device_id_type=MESH,
         )
 
-    def arrived(other):
-        for d in range(2):
+    per_z = NX * CAP
+
+    def gather(d):
+        def arrived(j, carry):
+            other = (me + j) % held
             pltpu.make_async_remote_copy(
                 src_ref=psend.at[d, other], dst_ref=drec.at[other, d],
                 send_sem=d_ss.at[d, 0], recv_sem=d_rs.at[d, other],
                 device_id={"expert": other}, device_id_type=MESH,
             ).wait_recv()
-
-    per_z = NX * CAP
-
-    def expert_block(turn, own):
+            return carry
+
+        lax.fori_loop(1, held, arrived, 0)
+
+        def sort(zs, carry):
+            block = drec[pl.ds(zs * NX, NX), d].reshape(NX * SLAB, width)
+            sorted_rows = mm(unpack[...], block).astype(BF16)
+            for f in range(NF):
+                rows[d, f, pl.ds(pl.multiple_of(zs * per_z, per_z), per_z), :] = sorted_rows[
+                    f * per_z : (f + 1) * per_z, :
+                ]
+            return carry
+
+        lax.fori_loop(0, NZ, sort, 0)
+
+    def hide(d, half):
+        gate = jnp.zeros((NZ * per_z, gu.shape[3]), F32)
+        up = jnp.zeros((NZ * per_z, gu.shape[3]), F32)
+        for f in range(NF):
+            part = rows[d, f]
+            gate = gate + mm(part, gu[half, 0, f * width : (f + 1) * width, :])
+            up = up + mm(part, gu[half, 1, f * width : (f + 1) * width, :])
+        return (gate / (1.0 + jnp.exp(-gate)) * up).astype(BF16)
+
+    def block_of(turn):
         zs, _ = peer(turn * NX)
-        for k in range(1 if own else 0, NX):
-            arrived(peer(turn * NX + k)[1])
-        block = drec[pl.ds(zs * NX, NX)].reshape(NX * 2 * SLAB, width)
-        rows = mm(unpack[...], block).astype(BF16)
-        result = jnp.zeros((2 * per_z, features), F32)
-        for half in range(2):
-            gate = jnp.zeros((2 * per_z, gu.shape[3]), F32)
-            up = jnp.zeros((2 * per_z, gu.shape[3]), F32)
-            for f in range(NF):
-                part = rows[f * 2 * per_z : (f + 1) * 2 * per_z, :]
-                gate = gate + mm(part, gu[half, 0, f * width : (f + 1) * width, :])
-                up = up + mm(part, gu[half, 1, f * width : (f + 1) * width, :])
-            hidden = (gate / (1.0 + jnp.exp(-gate)) * up).astype(BF16)
-            result = result + mm(hidden, dn[half])
-        mine[turn] = result[:per_z]
-        ysend[turn] = result[per_z:].astype(BF16)
+        return pl.ds(pl.multiple_of(zs * per_z, per_z), per_z)
+
+    def lend(turn, carry):
+        here = block_of(turn)
+        ysend[turn] = (mine[1, here, :] + mm(hid[here, :], dn[1])).astype(BF16)
         y_copy(turn).start()
+        return carry
 
     def back_copy(step):
         _, other = peer(step)
@@ -223,7 +242,7 @@
 
     def give_back(turn, own):
         y_copy(turn).wait_recv()
-        summed = (mine[turn] + yrecv[turn].astype(F32)).astype(BF16)
+        summed = (mine[0, block_of(turn), :] + yrecv[turn].astype(F32)).astype(BF16)
         tall = jnp.concatenate(
             [summed[:, f * width : (f + 1) * width] for f in range(NF)], axis=0
         )
@@ -233,18 +252,21 @@
         if own:
             rec[me] = zsend[turn, x]
 
-    expert_block(0, False)
-    expert_block(1, False)
+    for d in range(2):
+        gather(d)
+        mine[d] = mm(hide(d, 0), dn[0])
+    weight_copies[0].wait()
+    weight_copies[1].wait()
+    hid[...] = hide(1, 1)
+    weight_copies[2].wait()
+    lax.fori_loop(0, NZ, lend, 0)
+    mine[0] = mine[0] + mm(hide(0, 1), dn[1])
 
     def steady(turn, carry):
-        expert_block(turn, False)
-        give_back(turn - 2, False)
-        return carry
-
-    lax.fori_loop(2, NZ - 1, steady, 0)
-    expert_block(NZ - 1, True)
-    give_back(NZ - 3, False)
-    give_back(NZ - 2, False)
+        give_back(turn, False)
+        return carry
+
+    lax.fori_loop(0, NZ - 1, steady, 0)
     give_back(NZ - 1, True)
 
     def returned(j, carry):
@@ -293,15 +315,12 @@
 
 
 def moves():
-    per_z = NX * CAP
-    unpack = np.zeros((NF * 2 * per_z, NX * 2 * SLAB), np.float32)
     repack = np.zeros((NX * SLAB, NX * SLAB), np.float32)
     for f in range(NF):
         for xs in range(NX):
             for c in range(CAP):
-                for d in range(2):
-                    unpack[((f * 2 + d) * NX + xs) * CAP + c, ((xs * 2 + d) * NF + f) * CAP + c] = 1
                 repack[(xs * NF + f) * CAP + c, (f * NX + xs) * CAP + c] = 1
+    unpack = repack.T
     return jnp.asarray(unpack, BF16), jnp.asarray(repack, BF16)
 
 
@@ -329,7 +348,9 @@
             pltpu.VMEM((held, 2, SLAB, width), BF16),
             pltpu.VMEM((2, 2, features, units), BF16),
             pltpu.VMEM((2, units, features), BF16),
-            pltpu.VMEM((NZ, NX * CAP, features), F32),
+            pltpu.VMEM((2, NF, held * CAP, width), BF16),
+            pltpu.VMEM((2, held * CAP, features), F32),
+            pltpu.VMEM((held * CAP, units), BF16),
             pltpu.VMEM((NZ, NX * CAP, features), BF16),
             pltpu.VMEM((NZ, NX * CAP, features), BF16),
             pltpu.VMEM((NZ, NX, SLAB, width), BF16),
@@ -337,9 +358,9 @@
             pltpu.VMEM((held * SLAB, 2 * NF * tokens), BF16),
             pltpu.VMEM((NF, tokens, width), BF16),
             pltpu.VMEM((NF, tokens, width), BF16),
-            dma((2,)), dma((2,)), dma((2, held)), dma((2, held)), dma((2,)), dma((2,)),
+            dma((2,)), dma((2,)), dma((2, held)), dma((2, held)), dma((3,)), dma((3,)),
             dma((2,)), dma((NZ,)), dma((NZ,)), dma((held,)), dma((held,)),
-            dma((NF,)), dma((NF,)),
+            dma((NF,)), dma((NF,)), pltpu.SemaphoreType.REGULAR,
         ],
         compiler_params=pltpu.CompilerParams(
             collective_id=0, has_side_effects=True, vmem_limit_bytes=56 << 20

time: 167 us -> 157 us (0.940)
  the two profiles are of different devices: /device:TPU:1 before, /device:TPU:194 now
where the time goes in v3:
time: 157 us; the launch traced here: 156 us
  Pallas kernels  155 us (99%)
  local copies, waits for them, and re-layouts  1.88 us (1%)
    pallas_call x1, Pallas kernels, shards(): pl.pallas_call(kernel, out_shape=jax.ShapeDtypeStruct((tokens, features),...  155 us

profile of v3, /device:TPU:194, one launch (start us, length us, event | category | flops | bytes accessed | tf_op | source)
XLA Modules:
  0.0 156.4 jit_solution(5701073813738970696)
XLA Ops:
  0.0 154.5 %routed.1 = bf16[128,2048]{1,0:T(8,128)(2,1)} custom-call(bf16[128,2048]{1,0:T(8,128)(2,1)} %bitcast.13, bf16[1,2048]{1,0:T(2,128)(2,1)} %gain.1, f32[8,128]{1,0:T(8,128)} %bitcast.14, s32[8,128]{1,0:T(8,128)} %bitcast.15, bf16[2,2048,256]{2,1,0:T(8,128)(2,1)} %bitcast.11, bf16[256,2048]{1,0:T(8,128)(2,1)} %bitcast.12, ...), custom_call_target="tpu_custom_call" | custom-call | tf_op jit(solution)/shard_map/routed/pallas_call | solution.py:336
  154.5 1.9 %copy.10 = bf16[1,128,2048]{2,1,0:T(8,128)(2,1)} copy(bf16[1,128,2048]{2,1,0:T(8,128)(2,1)} %bitcast.10) | data formatting | bytes 1048576
